TPU v7x, 32 devices: a whole 2x2x4 slice. The times are simulated.
32 devices in a mesh: group: 2 (over y), tile: 4 (over x, core), seq: 4 (over z).
Axes of the slice: x: 2, y: 2, z: 4, core: 2. Of those that a mesh axis runs over, the one named last changes fastest.
Arguments:
- hidden: bfloat16 [8, 1024, 3072], P(('group', 'tile'), 'seq'), parts along dimension 0
- modulation: float32 [10, 3072], P('group'), parts along dimension 0, may hold values from -3 to 3
- w_qkv: bfloat16 [3072, 9216], P('tile', 'seq')
- w_out: bfloat16 [3072, 3072], P('seq', 'tile'), may hold values from -0.109375 to 0.109375
- w_head: bfloat16 [3072, 64], replicated, may hold values from -0.109375 to 0.109375
- latent: float32 [8, 1024, 64], P(('group', 'tile'), 'seq'), parts along dimension 0, may hold values from -6 to 6
- weights_int: int32 [8, 1024], P(('group', 'tile'), 'seq'), parts along dimension 0, may hold values from 1 to 8
- step_index: int32 [2], P('group'), parts along dimension 0, may hold values from 0 to 13
Outputs:
- stepped: float32 [8, 1024, 64], P(('group', 'tile'), 'seq'), parts along dimension 0
- clean: float32 [8, 1024, 64], P(('group', 'tile'), 'seq'), parts along dimension 0
There are 2 independent parts, one for each index of `group`. A program takes and returns all parts, laid end to end along the dimension named above; an argument that names none is the same for every part. Nothing has to cross between parts.
All inputs are finite; a program needn't handle non-finite values.
Results may differ from a plain program's by a relative error of at most 0.0055.
Values may be sent and summed in bfloat16 or wider, within the bound.
A program may use at most 64 MiB of HBM per device.

v0:
```python
import math
import jax
import jax.numpy as jnp
from jax import lax
from jax.sharding import PartitionSpec as P

HD = 128
NSTEPS = 28


def shifted(value, axis, steps):
    count = lax.axis_size(axis)
    leading, last = (max(0, -steps), min(count, count - steps))
    return lax.ppermute(value, axis, [(source, source + steps) for source in range(leading, last)])


def layer_norm(values):
    mean = jnp.mean(values, axis=-1, keepdims=True)
    centred = values - mean
    spread = jnp.mean(centred * centred, axis=-1, keepdims=True)
    return centred * lax.rsqrt(spread + 1e-06)


def root_norm(values):
    return values * lax.rsqrt(jnp.mean(values * values, axis=-1, keepdims=True) + 1e-06)


def noise_level(index, steps):
    level = 1.0 - index / steps
    return 3.0 * level / (1.0 + 2.0 * level)


def shards(hidden, modulation, w_qkv, w_out, w_head, latent, weights_int, step_index):
    local = hidden[0].astype(jnp.float32)
    norm_in = (layer_norm(local) * (1.0 + modulation[1]) + modulation[0]).astype(jnp.bfloat16)
    gathered = lax.all_gather(norm_in, "seq", axis=0, tiled=True)
    length = gathered.shape[0]
    heads_here = w_qkv.shape[1] // (3 * HD)
    projected = jnp.dot(
        gathered,
        lax.all_gather(w_qkv, "tile", axis=0, tiled=True),
        preferred_element_type=jnp.float32,
    )
    full_out = lax.all_gather(w_out, "tile", axis=1, tiled=True)
    projected = projected.reshape(length, heads_here, 3, HD)
    queries = root_norm(projected[:, :, 0]).astype(jnp.bfloat16)
    keys = root_norm(projected[:, :, 1]).astype(jnp.bfloat16)
    values = projected[:, :, 2].astype(jnp.bfloat16)
    block = min(512, length)
    scale = 1.0 / math.sqrt(HD)
    pieces = []
    for first in range(0, length, block):
        scores = (
            jnp.einsum(
                "qhe,khe->hqk",
                queries[first : first + block],
                keys,
                preferred_element_type=jnp.float32,
            )
            * scale
        )
        expo = jnp.exp(scores)
        probs = (expo / jnp.sum(expo, axis=-1, keepdims=True)).astype(jnp.bfloat16)
        pieces.append(
            jnp.einsum("hqk,khe->qhe", probs, values, preferred_element_type=jnp.float32).astype(
                jnp.bfloat16
            )
        )
    attended = jnp.concatenate(pieces, axis=0).reshape(length, heads_here * HD)
    summed = lax.psum_scatter(
        jnp.dot(attended, full_out, preferred_element_type=jnp.float32).astype(jnp.bfloat16),
        "seq",
        scatter_dimension=0,
        tiled=True,
    ).astype(jnp.float32)
    mixed = local + modulation[2] * summed
    norm_out = (layer_norm(mixed) * (1.0 + modulation[4]) + modulation[3]).astype(jnp.bfloat16)
    velocity = jnp.dot(norm_out, w_head, preferred_element_type=jnp.float32)
    index = step_index[0].astype(jnp.float32)
    now = noise_level(index, NSTEPS)
    after = noise_level(index + 1.0, NSTEPS)
    base = latent[0]
    weight = weights_int[0].astype(jnp.float32)
    moved = base + (after - now) * velocity
    guess = base - now * velocity
    weighted = jnp.concatenate([moved, guess], axis=1) * weight[:, None]
    seq_count = lax.axis_size("seq")
    place = lax.axis_index("seq")
    prev_tile = (
        shifted(weighted.astype(jnp.bfloat16), "tile", 1).astype(weighted.dtype),
        shifted(weight.astype(jnp.bfloat16), "tile", 1).astype(weight.dtype),
    )
    prev_sums, prev_weight = (
        shifted(prev_tile[0].astype(jnp.bfloat16), "seq", -(seq_count - 2)).astype(jnp.float32),
        shifted(prev_tile[1].astype(jnp.bfloat16), "seq", -(seq_count - 2)).astype(jnp.float32),
    )
    next_tile = (
        shifted(weighted.astype(jnp.bfloat16), "tile", -1).astype(weighted.dtype),
        shifted(weight.astype(jnp.bfloat16), "tile", -1).astype(weight.dtype),
    )
    next_sums, next_weight = (
        shifted(next_tile[0].astype(jnp.bfloat16), "seq", seq_count - 2).astype(jnp.float32),
        shifted(next_tile[1].astype(jnp.bfloat16), "seq", seq_count - 2).astype(jnp.float32),
    )
    take_prev = place < 2
    take_next = place >= seq_count - 2
    totals = weighted + jnp.where(take_prev, prev_sums, 0.0) + jnp.where(take_next, next_sums, 0.0)
    norms = weight + jnp.where(take_prev, prev_weight, 0.0) + jnp.where(take_next, next_weight, 0.0)
    joined = totals / norms[:, None]
    channels = velocity.shape[1]
    return (joined[None, :, :channels], joined[None, :, channels:])


def solution(mesh):
    in_specs = (
        P(("group", "tile"), "seq", None),
        P("group", None),
        P("tile", "seq"),
        P("seq", "tile"),
        P(),
        P(("group", "tile"), "seq", None),
        P(("group", "tile"), "seq"),
        P("group"),
    )
    out_specs = (P(("group", "tile"), "seq", None), P(("group", "tile"), "seq", None))
    return jax.shard_map(shards, mesh=mesh, in_specs=in_specs, out_specs=out_specs, check_vma=False)
```

profile of v0, /device:TPU:26, one launch (start us, length us, event | category | flops | bytes accessed | tf_op | source)
XLA Modules:
  0.0 437.2 jit_solution(16859526870282650366)
XLA Ops:
  10.8 2.0 fusion.8
  12.8 1.9 fusion.11
  16.3 112.1 %all-gather.4.cloned.1.call-done = bf16[1024,3072]{1,0:T(8,128)(2,1)} async-done(((bf16[256,3072]{1,0:T(8,128)(2,1)}), bf16[1024,3072]{1,0:T(8,128)(2,1)}) %all-gather.4.cloned.1.call-update) | async-done | bytes 6291472 | tf_op jit(solution)/shard_map/all_gather | solution.py:36
  128.4 92.7 %all-gather.6.cloned.1.call-done = bf16[3072,2304]{1,0:T(8,128)(2,1)} async-done(((bf16[768,2304]{1,0:T(8,128)(2,1)}), bf16[3072,2304]{1,0:T(8,128)(2,1)}) %all-gather.6.cloned.1.call-update) | async-done | bytes 14155792 | tf_op jit(solution)/shard_map/all_gather | solution.py:41
  221.1 19.6 %fusion.31 = f32[1024,2304]{0,1:T(8,128)S(1)} fusion(bf16[1024,3072]{1,0:T(8,128)(2,1)} %all-gather.4.cloned.1.call-done, bf16[3072,2304]{1,0:T(8,128)(2,1)} %all-gather.6.cloned.1.call-done), kind=kOutput, calls=%fused_computation.60 | convolution fusion | flops 14495514624 | bytes 29884416 | tf_op jit(solution)/shard_map/dot_general | solution.py:39
  240.7 3.5 copy-done.3
  244.2 2.0 slice.50
  246.3 3.6 copy.21
  249.9 2.9 fusion.12
  252.8 2.3 multiply_reduce_fusion.1
  256.2 8.2 %fusion = (f32[6,512]{1,0:T(8,128)S(1)}, f32[6,512,1024]{2,1,0:T(8,128)}) fusion(f32[1024,6,3,128]{0,3,2,1:T(8,128)} %bitcast.78, f32[1024,6]{0,1:T(8,128)S(1)} %add_rsqrt_fusion, bf16[1024,6,128]{2,0,1:T(8,128)(2,1)S(1)} %fusion.13), kind=kOutput, calls=%fused_computation.4 | convolution fusion | flops 813167616 | bytes 16560128 | tf_op jit(solution)/shard_map/qhe,khe->hqk/dot_general | solution.py:54
  264.5 2.7 fusion.1
  267.1 6.0 %fusion.19 = bf16[512,6,128]{0,2,1:T(8,128)(2,1)S(1)} fusion(f32[6,512,1024]{2,1,0:T(8,128)} %get-tuple-element.14, f32[6,512]{1,0:T(8,128)S(1)} %get-tuple-element.13, f32[1024,6,3,128]{0,3,2,1:T(8,128)S(1)} %bitcast.82), kind=kOutput, calls=%fused_computation.35 | convolution fusion | flops 815136768 | bytes 14958592 | tf_op jit(solution)/shard_map/hqk,khe->qhe/dot_general | solution.py:65
  273.1 2.9 fusion.20
  276.3 9.5 %convolution_convert_fusion = bf16[1024,3072]{1,0:T(8,128)(2,1)} fusion(bf16[1024,768]{0,1:T(8,128)(2,1)S(1)} %bitcast.84, bf16[768,3072]{1,0:T(8,128)(2,1)} %all-gather.8.cloned.1.call-done), kind=kOutput, calls=%fused_computation.8 | convolution fusion | flops 4834983936 | bytes 12582912 | tf_op jit(solution)/shard_map/dot_general | solution.py:71
  286.6 110.6 %reduce-scatter.2.cloned.1.call-done = bf16[256,3072]{1,0:T(8,128)(2,1)} async-done(((bf16[1024,3072]{1,0:T(8,128)(2,1)}), bf16[256,3072]{1,0:T(8,128)(2,1)}) %reduce-scatter.2.cloned.1.call-update) | async-done | bytes 1572880 | tf_op jit(solution)/shard_map/reduce_scatter | solution.py:70
  397.2 2.1 fusion.14
  401.3 1.9 collective-permute-start
  403.3 3.6 collective-permute-start.2
  406.9 1.9 collective-permute-start.4
  408.9 3.6 collective-permute-start.6
  412.5 2.9 collective-permute-start.5
  416.8 5.4 %collective-permute-start.1 = (bf16[256,128]{0,1:T(8,128)(2,1)S(1)}, bf16[256,128]{0,1:T(8,128)(2,1)S(1)}, u32[]{:S(2)}, u32[]{:S(2)}) collective-permute-start(bf16[256,128]{0,1:T(8,128)(2,1)S(1)} %collective-permute-done), channel_id=1, source_target_pairs={{2,0},{3,1},{6,4},{7,5},{10,8},{11,9},{14,12},{15,13},{18,16},{19,... | collective-permute-start | bytes 196616 | tf_op jit(solution)/shard_map/ppermute | solution.py:14
  424.1 5.9 %collective-permute-done.3 = bf16[256,128]{0,1:T(8,128)(2,1)S(1)} collective-permute-done((bf16[256,128]{0,1:T(8,128)(2,1)S(1)}, bf16[256,128]{0,1:T(8,128)(2,1)S(1)}, u32[]{:S(2)}, u32[]{:S(2)}) %collective-permute-start.3) | collective-permute-done | bytes 65568 | tf_op jit(solution)/shard_map/ppermute | solution.py:14
  (60 shorter events, 12.2 us)
Async XLA Ops:
  7.2 393.0 %copy-start = (bf16[3072,64]{0,1:T(8,128)(2,1)S(1)}, bf16[3072,64]{0,1:T(8,128)(2,1)}, u32[]{:S(2)}) copy-start(bf16[3072,64]{0,1:T(8,128)(2,1)} %param.12) | copy-start | bytes 1179652
  7.2 5.6 %copy-start.1 = (bf16[1,256,3072]{2,1,0:T(8,128)(2,1)S(1)}, bf16[1,256,3072]{2,1,0:T(8,128)(2,1)}, u32[]{:S(2)}) copy-start(bf16[1,256,3072]{2,1,0:T(8,128)(2,1)} %param.8) | copy-start | bytes 4718596
  7.2 121.2 %all-gather.4.cloned.1.call-start = ((), (), s32[]{:S(2)}) async-start(), calls=%async_computation.1 | async-start | bytes 7864320 | tf_op jit(solution)/shard_map/all_gather | solution.py:36
  14.8 206.3 %all-gather.6.cloned.1.call-start = ((), (), s32[]{:S(2)}) async-start(), calls=%async_computation.2 | async-start | bytes 17694720 | tf_op jit(solution)/shard_map/all_gather | solution.py:41
  15.5 260.8 %all-gather.8.cloned.1.call-start = ((), (), s32[]{:S(2)}) async-start(), calls=%async_computation.3 | async-start | bytes 5898240 | tf_op jit(solution)/shard_map/all_gather | solution.py:44
  16.3 381.0 %reduce-scatter.2.cloned.1.call-start = ((), (), s32[]{:S(2)}) async-start(), calls=%async_computation.4 | async-start | bytes 7864320 | tf_op jit(solution)/shard_map/reduce_scatter | solution.py:70
  240.7 3.6 copy-start.3
  249.9 5.3 %copy-start.2 = (f32[1024,6,1,128]{3,0,1,2:T(8,128)S(1)}, f32[1024,6,1,128]{3,0,1,2:T(8,128)}, u32[]{:S(2)}) copy-start(f32[1024,6,1,128]{3,0,1,2:T(8,128)} %copy.21) | copy-start | bytes 9437188
  255.2 9.2 %slice-start = ((s8[9437184]{0:T(1024)(128)(4,1)}), s8[4194304]{0:T(1024)(128)(4,1)S(1)}, s32[]{:S(2)}) async-start(s8[9437184]{0:T(1024)(128)(4,1)} %bitcast.79), calls=%async_computation.5 | async-start | bytes 8388608
  256.2 8.3 %slice-start.1 = ((s8[9437184]{0:T(1024)(128)(4,1)}), s8[4194304]{0:T(1024)(128)(4,1)S(1)}, s32[]{:S(2)}) async-start(s8[9437184]{0:T(1024)(128)(4,1)} %bitcast.79), calls=%async_computation.6 | async-start | bytes 8388608
  256.2 8.2 %slice-start.2 = ((s8[9437184]{0:T(1024)(128)(4,1)}), s8[1048576]{0:T(1024)(128)(4,1)S(1)}, s32[]{:S(2)}) async-start(s8[9437184]{0:T(1024)(128)(4,1)} %bitcast.79), calls=%async_computation.7 | async-start | bytes 2097152
  285.8 0.7 copy-start.7
  397.2 2.1 copy-start.4
  397.2 3.0 copy-start.5
  397.2 3.0 copy-start.6
  397.2 3.0 copy-start.8
  401.3 15.4 %collective-permute-start = (bf16[256,128]{0,1:T(8,128)(2,1)S(1)}, bf16[256,128]{0,1:T(8,128)(2,1)S(1)}, u32[]{:S(2)}, u32[]{:S(2)}) collective-permute-start(bf16[256,128]{0,1:T(8,128)(2,1)S(1)} %fusion.27), channel_id=1, source_target_pairs={{0,4},{4,8},{8,12},{1,5},{5,9},{9,13},{2,6},{6,10},{10,14},{3,7},{... | collective-permute-start | bytes 196616 | tf_op jit(solution)/shard_map/ppermute | solution.py:14
  403.3 19.0 %collective-permute-start.2 = (bf16[256,128]{0,1:T(8,128)(2,1)S(1)}, bf16[256,128]{0,1:T(8,128)(2,1)S(1)}, u32[]{:S(2)}, u32[]{:S(2)}) collective-permute-start(bf16[256,128]{0,1:T(8,128)(2,1)S(1)} %fusion.27), channel_id=1, source_target_pairs={{4,0},{8,4},{12,8},{5,1},{9,5},{13,9},{6,2},{10,6},{14,10},{7,3},{... | collective-permute-start | bytes 196616 | tf_op jit(solution)/shard_map/ppermute | solution.py:14
  406.9 5.6 %collective-permute-start.4 = (bf16[256]{0:T(256)(128)(2,1)S(1)}, bf16[256]{0:T(256)(128)(2,1)S(1)}, u32[]{:S(2)}, u32[]{:S(2)}) collective-permute-start(bf16[256]{0:T(256)(128)(2,1)S(1)} %convert_element_type.109), channel_id=1, source_target_pairs={{0,4},{4,8},{8,12},{1,5},{5,9},{9,13},{2,6},{6,10},{10,14},{3,7},{... | collective-permute-start | bytes 1544 | tf_op jit(solution)/shard_map/ppermute | solution.py:14
  408.9 6.6 %collective-permute-start.6 = (bf16[256]{0:T(256)(128)(2,1)S(1)}, bf16[256]{0:T(256)(128)(2,1)S(1)}, u32[]{:S(2)}, u32[]{:S(2)}) collective-permute-start(bf16[256]{0:T(256)(128)(2,1)S(1)} %convert_element_type.109), channel_id=1, source_target_pairs={{4,0},{8,4},{12,8},{5,1},{9,5},{13,9},{6,2},{10,6},{14,10},{7,3},{... | collective-permute-start | bytes 1544 | tf_op jit(solution)/shard_map/ppermute | solution.py:14
  412.5 11.0 %collective-permute-start.5 = (bf16[256]{0:T(256)(128)(2,1)S(1)}, bf16[256]{0:T(256)(128)(2,1)S(1)}, u32[]{:S(2)}, u32[]{:S(2)}) collective-permute-start(bf16[256]{0:T(256)(128)(2,1)S(1)} %collective-permute-done.4), channel_id=1, source_target_pairs={{2,0},{3,1},{6,4},{7,5},{10,8},{11,9},{14,12},{15,13},{18,16},{19,... | collective-permute-start | bytes 1544 | tf_op jit(solution)/shard_map/ppermute | solution.py:14
  415.5 8.1 %collective-permute-start.7 = (bf16[256]{0:T(256)(128)(2,1)S(1)}, bf16[256]{0:T(256)(128)(2,1)S(1)}, u32[]{:S(2)}, u32[]{:S(2)}) collective-permute-start(bf16[256]{0:T(256)(128)(2,1)S(1)} %collective-permute-done.6), channel_id=1, source_target_pairs={{0,2},{1,3},{4,6},{5,7},{8,10},{9,11},{12,14},{13,15},{16,18},{17,... | collective-permute-start | bytes 1544 | tf_op jit(solution)/shard_map/ppermute | solution.py:14
  416.8 7.3 %collective-permute-start.1 = (bf16[256,128]{0,1:T(8,128)(2,1)S(1)}, bf16[256,128]{0,1:T(8,128)(2,1)S(1)}, u32[]{:S(2)}, u32[]{:S(2)}) collective-permute-start(bf16[256,128]{0,1:T(8,128)(2,1)S(1)} %collective-permute-done), channel_id=1, source_target_pairs={{2,0},{3,1},{6,4},{7,5},{10,8},{11,9},{14,12},{15,13},{18,16},{19,... | collective-permute-start | bytes 196616 | tf_op jit(solution)/shard_map/ppermute | solution.py:14
  422.2 7.7 %collective-permute-start.3 = (bf16[256,128]{0,1:T(8,128)(2,1)S(1)}, bf16[256,128]{0,1:T(8,128)(2,1)S(1)}, u32[]{:S(2)}, u32[]{:S(2)}) collective-permute-start(bf16[256,128]{0,1:T(8,128)(2,1)S(1)} %collective-permute-done.2), channel_id=1, source_target_pairs={{0,2},{1,3},{4,6},{5,7},{8,10},{9,11},{12,14},{13,15},{16,18},{17,... | collective-permute-start | bytes 196616 | tf_op jit(solution)/shard_map/ppermute | solution.py:14
Sparse Core Ops, SparseCore 0:
  14.9 113.4 all-gather.3
  129.9 91.1 all-gather.5
  222.6 37.4 all-gather.7
  286.0 111.1 reduce-scatter.1
where the time goes:
time: 438 us; the launch traced here: 437 us
  waiting for transfers between devices  323 us (74%)
  matrix products  50 us (11%)
  starting transfers between devices  22.2 us (5%)
  other arithmetic  17 us (4%)
  between operations  14.9 us (3%)
  local copies, waits for them, and re-layouts  9.9 us (2%)
    all_gather x1, waiting for transfers between devices, shards(): gathered = lax.all_gather(norm_in, 'seq', axis=0, tiled=True)  112 us
    reduce_scatter x1, waiting for transfers between devices, shards(): lax.psum_scatter(jnp.dot(attended, full_out, preferred_element_type=jnp.f...  111 us
    all_gather x1, waiting for transfers between devices, shards(): lax.all_gather(w_qkv, 'tile', axis=0, tiled=True)  92.7 us
    ppermute x8, starting transfers between devices, shifted(): lax.ppermute(value, axis, [(source, source + steps) for source in range(l...  22.1 us
    dot_general x1, matrix products, shards(): jnp.dot(gathered, lax.all_gather(w_qkv, 'tile', axis=0, tiled=True), pref...  19.6 us
    dot_general x2, matrix products, shards(): jnp.einsum('qhe,khe->hqk', queries[first:first + block], keys, preferred_...  10.9 us
    dot_general x1, matrix products, shards(): jnp.dot(attended, full_out, preferred_element_type=jnp.float32)  9.54 us
    dot_general x2, matrix products, shards(): jnp.einsum('hqk,khe->qhe', probs, values, preferred_element_type=jnp.floa...  8.92 us
  transfers between devices with their start and end apart: 12, of which 5 were waited for; matrix products, arithmetic and copies ran while one was open for 12% of the time, Pallas kernels for 0%

commit v1 on v0

--- a/solution.py
+++ b/solution.py
@@ -33,7 +33,21 @@
 def shards(hidden, modulation, w_qkv, w_out, w_head, latent, weights_int, step_index):
     local = hidden[0].astype(jnp.float32)
     norm_in = (layer_norm(local) * (1.0 + modulation[1]) + modulation[0]).astype(jnp.bfloat16)
-    gathered = lax.all_gather(norm_in, "seq", axis=0, tiled=True)
+    block_next, block_out, found_now = (
+        lax.axis_size("seq"),
+        lax.axis_index("seq"),
+        norm_in.shape[0],
+    )
+    next_value, a_now = (norm_in, 1)
+    while a_now < block_next:
+        pile = []
+        for dev_i in [*range(block_next)]:
+            pile.append((dev_i, (dev_i - a_now) % block_next))
+        next_value = jnp.concatenate(
+            [next_value, lax.ppermute(next_value, axis_name="seq", perm=pile)], axis=0
+        )
+        a_now = 2 * a_now
+    gathered = jnp.roll(next_value, shift=block_out * found_now, axis=0)
     length = gathered.shape[0]
     heads_here = w_qkv.shape[1] // (3 * HD)
     projected = jnp.dot(

time: 438 us -> 414 us (0.945)
  waiting for transfers between devices: 323 us -> 290 us
  local copies, waits for them, and re-layouts: 9.9 us -> 21.8 us
    ppermute x0 -> x2, waiting for transfers between devices: none -> 172 us  [shards(): lax.ppermute(next_value, axis_name='seq', perm=pile)]
    all_gather x1 -> x0, waiting for transfers between devices: 112 us -> none  [shards(): gathered = lax.all_gather(norm_in, 'seq', axis=0, tiled=True)]
    all_gather x1, waiting for transfers between devices: 92.7 us -> 0.01 us  [shards(): lax.all_gather(w_qkv, 'tile', axis=0, tiled=True)]
    unnamed x25 -> x35, local copies, waits for them, and re-layouts: 7.19 us -> 15.3 us
  transfers between devices with their start and end apart: 12 -> 13, of which waited for: 5 -> 5; matrix products, arithmetic and copies ran while one was open for 12% -> 16% of each run, Pallas kernels for 0% -> 0%
where the time goes in v1:
time: 414 us
  waiting for transfers between devices  290 us (70%)
  matrix products  50 us (12%)
  starting transfers between devices  22.7 us (5%)
  local copies, waits for them, and re-layouts  21.8 us (5%)
  between operations  14.9 us (4%)
  other arithmetic  14.7 us (4%)
    ppermute x2, waiting for transfers between devices, shards(): lax.ppermute(next_value, axis_name='seq', perm=pile)  172 us
    reduce_scatter x1, waiting for transfers between devices, shards(): lax.psum_scatter(jnp.dot(attended, full_out, preferred_element_type=jnp.f...  111 us
    ppermute x8, starting transfers between devices, shifted(): lax.ppermute(value, axis, [(source, source + steps) for source in range(l...  22.1 us
    dot_general x1, matrix products, shards(): jnp.dot(gathered, lax.all_gather(w_qkv, 'tile', axis=0, tiled=True), pref...  19.6 us
    unnamed x35, local copies, waits for them, and re-layouts  15.3 us
    dot_general x2, matrix products, shards(): jnp.einsum('qhe,khe->hqk', queries[first:first + block], keys, preferred_...  10.9 us
    dot_general x1, matrix products, shards(): jnp.dot(attended, full_out, preferred_element_type=jnp.float32)  9.6 us
    dot_general x2, matrix products, shards(): jnp.einsum('hqk,khe->qhe', probs, values, preferred_element_type=jnp.floa...  8.92 us
  transfers between devices with their start and end apart: 13, of which 5 were waited for; matrix products, arithmetic and copies ran while one was open for 16% of the time, Pallas kernels for 0%

profile of v1, /device:TPU:26, one launch (start us, length us, event | category | flops | bytes accessed | tf_op | source)
XLA Modules:
  0.0 413.9 jit_solution(17452144946436750811)
XLA Ops:
  12.4 37.5 %collective-permute-done = bf16[256,3072]{1,0:T(8,128)(2,1)S(1)} collective-permute-done((bf16[256,3072]{1,0:T(8,128)(2,1)S(1)}, bf16[256,3072]{1,0:T(8,128)(2,1)S(1)}, u32[]{:S(2)}, u32[]{:S(2)}) %collective-permute-start) | collective-permute-done | bytes 1572896 | tf_op jit(solution)/shard_map/ppermute | solution.py:47
  49.9 1.9 pad_maximum_fusion
  53.2 134.5 %collective-permute-done.1 = bf16[512,3072]{1,0:T(8,128)(2,1)} collective-permute-done((bf16[512,3072]{1,0:T(8,128)(2,1)}, bf16[512,3072]{1,0:T(8,128)(2,1)}, u32[]{:S(2)}, u32[]{:S(2)}) %collective-permute-start.1) | collective-permute-done | bytes 3145760 | tf_op jit(solution)/shard_map/ppermute | solution.py:47
  187.7 3.7 constant_dynamic-update-slice_fusion.3
  194.0 3.8 constant_dynamic-update-slice_fusion
  197.7 19.6 %fusion.2 = f32[1024,2304]{0,1:T(8,128)S(1)} fusion(bf16[3072,2304]{1,0:T(8,128)(2,1)} %all-gather.3.cloned.1.call-done, bf16[2048,3072]{1,0:T(8,128)(2,1)} %constant_dynamic-update-slice_fusion, s32[]{:T(128)S(6)} %select_n.42), kind=kOutput, calls=%fused_computation.6 | convolution fusion | flops 14495514624 | bytes 29884420 | tf_op jit(solution)/shard_map/dot_general | solution.py:53
  217.3 3.5 copy-done.3
  220.9 2.1 slice.50
  223.0 3.5 copy.21
  226.5 2.9 fusion.14
  229.5 2.3 multiply_reduce_fusion.1
  232.8 8.2 %fusion = (f32[6,512]{1,0:T(8,128)S(1)}, f32[6,512,1024]{2,1,0:T(8,128)}) fusion(f32[1024,6,3,128]{0,3,2,1:T(8,128)} %bitcast.78, f32[1024,6]{0,1:T(8,128)S(1)} %add_rsqrt_fusion, bf16[1024,6,128]{2,0,1:T(8,128)(2,1)S(1)} %fusion.15), kind=kOutput, calls=%fused_computation.4 | convolution fusion | flops 813167616 | bytes 16560128 | tf_op jit(solution)/shard_map/qhe,khe->hqk/dot_general | solution.py:68
  241.0 2.7 fusion.1
  243.7 6.0 %fusion.21 = bf16[512,6,128]{0,2,1:T(8,128)(2,1)S(1)} fusion(f32[6,512,1024]{2,1,0:T(8,128)} %get-tuple-element.16, f32[6,512]{1,0:T(8,128)S(1)} %get-tuple-element.15, f32[1024,6,3,128]{0,3,2,1:T(8,128)S(1)} %bitcast.82), kind=kOutput, calls=%fused_computation.38 | convolution fusion | flops 815136768 | bytes 14958592 | tf_op jit(solution)/shard_map/hqk,khe->qhe/dot_general | solution.py:79
  249.7 2.9 fusion.22
  252.9 9.6 %convolution_convert_fusion = bf16[1024,3072]{1,0:T(8,128)(2,1)} fusion(bf16[1024,768]{0,1:T(8,128)(2,1)S(1)} %bitcast.84, bf16[768,3072]{1,0:T(8,128)(2,1)} %all-gather.5.cloned.1.call-done), kind=kOutput, calls=%fused_computation.10 | convolution fusion | flops 4834983936 | bytes 12582912 | tf_op jit(solution)/shard_map/dot_general | solution.py:85
  263.3 110.6 %reduce-scatter.2.cloned.1.call-done = bf16[256,3072]{1,0:T(8,128)(2,1)} async-done(((bf16[1024,3072]{1,0:T(8,128)(2,1)}), bf16[256,3072]{1,0:T(8,128)(2,1)}) %reduce-scatter.2.cloned.1.call-update) | async-done | bytes 1572880 | tf_op jit(solution)/shard_map/reduce_scatter | solution.py:84
  373.9 2.1 fusion.16
  378.0 1.9 collective-permute-start.2
  379.9 3.6 collective-permute-start.4
  385.5 3.6 collective-permute-start.8
  389.2 2.9 collective-permute-start.7
  393.4 5.4 %collective-permute-start.3 = (bf16[256,128]{0,1:T(8,128)(2,1)S(1)}, bf16[256,128]{0,1:T(8,128)(2,1)S(1)}, u32[]{:S(2)}, u32[]{:S(2)}) collective-permute-start(bf16[256,128]{0,1:T(8,128)(2,1)S(1)} %collective-permute-done.2), channel_id=1, source_target_pairs={{2,0},{3,1},{6,4},{7,5},{10,8},{11,9},{14,12},{15,13},{18,16},{19,... | collective-permute-start | bytes 196616 | tf_op jit(solution)/shard_map/ppermute | solution.py:14
  400.8 5.9 %collective-permute-done.5 = bf16[256,128]{0,1:T(8,128)(2,1)S(1)} collective-permute-done((bf16[256,128]{0,1:T(8,128)(2,1)S(1)}, bf16[256,128]{0,1:T(8,128)(2,1)S(1)}, u32[]{:S(2)}, u32[]{:S(2)}) %collective-permute-start.5) | collective-permute-done | bytes 65568 | tf_op jit(solution)/shard_map/ppermute | solution.py:14
  (73 shorter events, 18.0 us)
Async XLA Ops:
  7.2 369.7 %copy-start = (bf16[3072,64]{0,1:T(8,128)(2,1)S(1)}, bf16[3072,64]{0,1:T(8,128)(2,1)}, u32[]{:S(2)}) copy-start(bf16[3072,64]{0,1:T(8,128)(2,1)} %param.12) | copy-start | bytes 1179652
  7.2 190.5 %all-gather.3.cloned.1.call-start = ((), (), s32[]{:S(2)}) async-start(), calls=%async_computation.1 | async-start | bytes 17694720 | tf_op jit(solution)/shard_map/all_gather | solution.py:55
  7.9 244.9 %all-gather.5.cloned.1.call-start = ((), (), s32[]{:S(2)}) async-start(), calls=%async_computation.2 | async-start | bytes 5898240 | tf_op jit(solution)/shard_map/all_gather | solution.py:58
  12.0 39.9 %copy-start.4 = (bf16[256,3072]{1,0:T(8,128)(2,1)}, bf16[256,3072]{1,0:T(8,128)(2,1)S(1)}, u32[]{:S(2)}) copy-start(bf16[256,3072]{1,0:T(8,128)(2,1)S(1)} %get-tuple-element.3) | copy-start | bytes 4718596
  12.0 37.9 %collective-permute-start = (bf16[256,3072]{1,0:T(8,128)(2,1)S(1)}, bf16[256,3072]{1,0:T(8,128)(2,1)S(1)}, u32[]{:S(2)}, u32[]{:S(2)}) collective-permute-start(bf16[256,3072]{1,0:T(8,128)(2,1)S(1)} %get-tuple-element.3), channel_id=1, source_target_pairs={{0,3},{1,0},{2,1},{3,2},{4,7},{5,4},{6,5},{7,6},{8,11},{9,8},{10,9... | collective-permute-start | bytes 4718600 | tf_op jit(solution)/shard_map/ppermute | solution.py:47
  51.9 135.8 %collective-permute-start.1 = (bf16[512,3072]{1,0:T(8,128)(2,1)}, bf16[512,3072]{1,0:T(8,128)(2,1)}, u32[]{:S(2)}, u32[]{:S(2)}) collective-permute-start(bf16[512,3072]{1,0:T(8,128)(2,1)} %pad_maximum_fusion), channel_id=1, source_target_pairs={{0,2},{1,3},{2,0},{3,1},{4,6},{5,7},{6,4},{7,5},{8,10},{9,11},{10,... | collective-permute-start | bytes 9437192 | tf_op jit(solution)/shard_map/ppermute | solution.py:47
  51.9 322.0 %reduce-scatter.2.cloned.1.call-start = ((), (), s32[]{:S(2)}) async-start(), calls=%async_computation.3 | async-start | bytes 7864320 | tf_op jit(solution)/shard_map/reduce_scatter | solution.py:84
  53.2 138.2 %copy-start.5 = (bf16[256,3072]{1,0:T(8,128)(2,1)S(1)}, bf16[256,3072]{1,0:T(8,128)(2,1)}, u32[]{:S(2)}) copy-start(bf16[256,3072]{1,0:T(8,128)(2,1)} %copy-done.4) | copy-start | bytes 4718596
  217.3 3.6 copy-start.3
  226.5 5.3 %copy-start.2 = (f32[1024,6,1,128]{3,0,1,2:T(8,128)S(1)}, f32[1024,6,1,128]{3,0,1,2:T(8,128)}, u32[]{:S(2)}) copy-start(f32[1024,6,1,128]{3,0,1,2:T(8,128)} %copy.21) | copy-start | bytes 9437188
  231.8 9.2 %slice-start = ((s8[9437184]{0:T(1024)(128)(4,1)}), s8[4194304]{0:T(1024)(128)(4,1)S(1)}, s32[]{:S(2)}) async-start(s8[9437184]{0:T(1024)(128)(4,1)} %bitcast.79), calls=%async_computation.4 | async-start | bytes 8388608
  232.8 8.2 %slice-start.1 = ((s8[9437184]{0:T(1024)(128)(4,1)}), s8[4194304]{0:T(1024)(128)(4,1)S(1)}, s32[]{:S(2)}) async-start(s8[9437184]{0:T(1024)(128)(4,1)} %bitcast.79), calls=%async_computation.5 | async-start | bytes 8388608
  232.8 8.2 %slice-start.2 = ((s8[9437184]{0:T(1024)(128)(4,1)}), s8[1048576]{0:T(1024)(128)(4,1)S(1)}, s32[]{:S(2)}) async-start(s8[9437184]{0:T(1024)(128)(4,1)} %bitcast.79), calls=%async_computation.6 | async-start | bytes 2097152
  373.9 3.0 copy-start.8
  373.9 3.0 copy-start.9
  373.9 3.0 copy-start.11
  378.0 15.4 %collective-permute-start.2 = (bf16[256,128]{0,1:T(8,128)(2,1)S(1)}, bf16[256,128]{0,1:T(8,128)(2,1)S(1)}, u32[]{:S(2)}, u32[]{:S(2)}) collective-permute-start(bf16[256,128]{0,1:T(8,128)(2,1)S(1)} %fusion.29), channel_id=1, source_target_pairs={{0,4},{4,8},{8,12},{1,5},{5,9},{9,13},{2,6},{6,10},{10,14},{3,7},{... | collective-permute-start | bytes 196616 | tf_op jit(solution)/shard_map/ppermute | solution.py:14
  379.9 19.0 %collective-permute-start.4 = (bf16[256,128]{0,1:T(8,128)(2,1)S(1)}, bf16[256,128]{0,1:T(8,128)(2,1)S(1)}, u32[]{:S(2)}, u32[]{:S(2)}) collective-permute-start(bf16[256,128]{0,1:T(8,128)(2,1)S(1)} %fusion.29), channel_id=1, source_target_pairs={{4,0},{8,4},{12,8},{5,1},{9,5},{13,9},{6,2},{10,6},{14,10},{7,3},{... | collective-permute-start | bytes 196616 | tf_op jit(solution)/shard_map/ppermute | solution.py:14
  383.6 5.6 %collective-permute-start.6 = (bf16[256]{0:T(256)(128)(2,1)S(1)}, bf16[256]{0:T(256)(128)(2,1)S(1)}, u32[]{:S(2)}, u32[]{:S(2)}) collective-permute-start(bf16[256]{0:T(256)(128)(2,1)S(1)} %convert_element_type.109), channel_id=1, source_target_pairs={{0,4},{4,8},{8,12},{1,5},{5,9},{9,13},{2,6},{6,10},{10,14},{3,7},{... | collective-permute-start | bytes 1544 | tf_op jit(solution)/shard_map/ppermute | solution.py:14
  385.5 6.6 %collective-permute-start.8 = (bf16[256]{0:T(256)(128)(2,1)S(1)}, bf16[256]{0:T(256)(128)(2,1)S(1)}, u32[]{:S(2)}, u32[]{:S(2)}) collective-permute-start(bf16[256]{0:T(256)(128)(2,1)S(1)} %convert_element_type.109), channel_id=1, source_target_pairs={{4,0},{8,4},{12,8},{5,1},{9,5},{13,9},{6,2},{10,6},{14,10},{7,3},{... | collective-permute-start | bytes 1544 | tf_op jit(solution)/shard_map/ppermute | solution.py:14
  389.2 11.0 %collective-permute-start.7 = (bf16[256]{0:T(256)(128)(2,1)S(1)}, bf16[256]{0:T(256)(128)(2,1)S(1)}, u32[]{:S(2)}, u32[]{:S(2)}) collective-permute-start(bf16[256]{0:T(256)(128)(2,1)S(1)} %collective-permute-done.6), channel_id=1, source_target_pairs={{2,0},{3,1},{6,4},{7,5},{10,8},{11,9},{14,12},{15,13},{18,16},{19,... | collective-permute-start | bytes 1544 | tf_op jit(solution)/shard_map/ppermute | solution.py:14
  392.1 8.1 %collective-permute-start.9 = (bf16[256]{0:T(256)(128)(2,1)S(1)}, bf16[256]{0:T(256)(128)(2,1)S(1)}, u32[]{:S(2)}, u32[]{:S(2)}) collective-permute-start(bf16[256]{0:T(256)(128)(2,1)S(1)} %collective-permute-done.8), channel_id=1, source_target_pairs={{0,2},{1,3},{4,6},{5,7},{8,10},{9,11},{12,14},{13,15},{16,18},{17,... | collective-permute-start | bytes 1544 | tf_op jit(solution)/shard_map/ppermute | solution.py:14
  393.4 7.3 %collective-permute-start.3 = (bf16[256,128]{0,1:T(8,128)(2,1)S(1)}, bf16[256,128]{0,1:T(8,128)(2,1)S(1)}, u32[]{:S(2)}, u32[]{:S(2)}) collective-permute-start(bf16[256,128]{0,1:T(8,128)(2,1)S(1)} %collective-permute-done.2), channel_id=1, source_target_pairs={{2,0},{3,1},{6,4},{7,5},{10,8},{11,9},{14,12},{15,13},{18,16},{19,... | collective-permute-start | bytes 196616 | tf_op jit(solution)/shard_map/ppermute | solution.py:14
  398.9 7.7 %collective-permute-start.5 = (bf16[256,128]{0,1:T(8,128)(2,1)S(1)}, bf16[256,128]{0,1:T(8,128)(2,1)S(1)}, u32[]{:S(2)}, u32[]{:S(2)}) collective-permute-start(bf16[256,128]{0,1:T(8,128)(2,1)S(1)} %collective-permute-done.4), channel_id=1, source_target_pairs={{0,2},{1,3},{4,6},{5,7},{8,10},{9,11},{12,14},{13,15},{16,18},{17,... | collective-permute-start | bytes 196616 | tf_op jit(solution)/shard_map/ppermute | solution.py:14
  (4 other events, 6.6 us)
Sparse Core Ops, SparseCore 0:
  9.6 91.0 all-gather.2
  102.2 37.4 all-gather.4
  262.6 111.2 reduce-scatter.1
